TPU v7x, 256 devices: a whole 4x4x8 slice. The times are simulated.
256 devices in a mesh: section: 8 (over y_lo, x), dp: 32 (over y_hi, z, core).
Axes of the slice: x: 4, y: 4 (y_hi: 2, y_lo: 2; y = y_hi * 2 + y_lo), z: 8, core: 2. Of those that a mesh axis runs over, the one named last changes fastest.
Arguments:
- nbr_embed: bfloat16 [32, 4, 128, 896], P('dp', None, 'section'), may hold values from -140 to 140
- enc_weight: bfloat16 [896, 896], replicated, may hold values from -0.1875 to 0.1875
- enc_gain: float32 [896], replicated, may hold values from 0.1 to 1.9
- kv_weight: bfloat16 [8, 4096, 896], P('section'), may hold values from -0.1875 to 0.1875
- queries: bfloat16 [8, 4096, 2048], P('section', 'dp'), may hold values from -6 to 6
- pos_bias: bfloat16 [8, 16, 64, 256], P('section'), may hold values from -8 to 240
- nbr_ids: int32 [32, 2, 2], P('dp'), may hold values from 0 to 3
- ctx_grad: bfloat16 [8, 4096, 2048], P('section', 'dp'), may hold values from -12 to 12
Outputs:
- q_grad: bfloat16 [8, 4096, 2048], P('section', 'dp')
- kv_weight_grad: float32 [8, 4096, 896], P('section', 'dp')
- enc_weight_grad: float32 [896, 896], P('section')
- enc_gain_grad: float32 [896], replicated
- embed_grad: bfloat16 [32, 4, 128, 896], P('dp', None, 'section')
All inputs are finite; a program needn't handle non-finite values.
Results may differ from a plain program's by a relative error of at most 0.02.
Values may be sent and summed in bfloat16 or wider, within the bound.
A program may use at most 128 MiB of HBM per device.

v0:
```python
import math

import jax
import jax.numpy as jnp
from jax import lax
from jax.sharding import PartitionSpec as P

HEADS = 16
HEAD = 128
ENC_D = 896
BLOCK = 64
NBR = 2
NLEN = 128
TOK_DEV = 128
NSET = 4


eps_norm = 1e-06


def attend_layer(weights, encoded_all, query_blk, bias_blk, ids_blk, grad_blk):
    head_width = HEADS * HEAD
    key_rows = NBR * NLEN
    blocks = TOK_DEV // BLOCK
    factor = 1.0 / math.sqrt(HEAD)
    projected = lax.dot_general(
        encoded_all, weights, (((1,), (1,)), ((), ())), preferred_element_type=jnp.float32
    ).astype(jnp.bfloat16)
    projected = projected.reshape(NSET, NLEN, 2 * head_width)
    selector = (ids_blk[:, :, None] == jnp.arange(NSET, dtype=jnp.int32)[None, None, :]).astype(
        jnp.bfloat16
    )
    chosen = jnp.einsum(
        "cne,eld->cnld", selector, projected, preferred_element_type=jnp.float32
    ).astype(jnp.bfloat16)
    chosen = chosen.reshape(blocks, key_rows, 2 * head_width)
    keys_all = chosen[:, :, :head_width].reshape(blocks, key_rows, HEADS, HEAD)
    values_all = chosen[:, :, head_width:].reshape(blocks, key_rows, HEADS, HEAD)
    query_all = query_blk.reshape(blocks, BLOCK, HEADS, HEAD)
    upstream = grad_blk.reshape(blocks, BLOCK, HEADS, HEAD)
    scores = (
        jnp.einsum("cqhd,ckhd->chqk", query_all, keys_all, preferred_element_type=jnp.float32)
        * factor
    )
    scores = scores + bias_blk.astype(jnp.float32)[None]
    row_peak = jnp.max(scores, axis=-1, keepdims=True)
    exp_scores = jnp.exp(scores - row_peak)
    attn_probs = exp_scores / jnp.sum(exp_scores, axis=-1, keepdims=True)
    probs_low = attn_probs.astype(jnp.bfloat16)
    grad_probs = jnp.einsum(
        "cqhd,ckhd->chqk", upstream, values_all, preferred_element_type=jnp.float32
    )
    row_inner = jnp.sum(attn_probs * grad_probs, axis=-1, keepdims=True)
    grad_scores = (attn_probs * (grad_probs - row_inner)).astype(jnp.bfloat16)
    grad_query = (
        jnp.einsum("chqk,ckhd->cqhd", grad_scores, keys_all, preferred_element_type=jnp.float32)
        * factor
    )
    grad_query = grad_query.astype(jnp.bfloat16).reshape(TOK_DEV, head_width)
    grad_keys = (
        jnp.einsum("chqk,cqhd->ckhd", grad_scores, query_all, preferred_element_type=jnp.float32)
        * factor
    )
    grad_values = jnp.einsum(
        "chqk,cqhd->ckhd", probs_low, upstream, preferred_element_type=jnp.float32
    )
    grad_chosen = jnp.concatenate(
        [
            grad_keys.reshape(blocks, key_rows, head_width),
            grad_values.reshape(blocks, key_rows, head_width),
        ],
        axis=-1,
    )
    grad_chosen = grad_chosen.reshape(blocks, NBR, NLEN, 2 * head_width)
    grad_set = jnp.einsum("cne,cnld->eld", selector.astype(jnp.float32), grad_chosen).astype(
        jnp.bfloat16
    )
    return (grad_query, grad_set.reshape(NSET * NLEN, 2 * head_width))


def body(nbr_embed, enc_weight, enc_gain, kv_weight, queries, pos_bias, nbr_ids, ctx_grad):
    local_rows = nbr_embed[0].reshape(-1, ENC_D)
    mixed_rows = local_rows.astype(jnp.float32) + jnp.dot(
        local_rows, enc_weight, preferred_element_type=jnp.float32
    )
    inverse = lax.rsqrt(jnp.mean(mixed_rows * mixed_rows, axis=-1, keepdims=True) + eps_norm)
    normed = mixed_rows * inverse
    encoded_local = (normed * enc_gain[None, :]).astype(jnp.bfloat16).reshape(NSET, -1, ENC_D)
    encoded_all = lax.all_gather(encoded_local, "section", axis=1, tiled=True).reshape(
        NSET * NLEN, ENC_D
    )
    weights = kv_weight[0]
    grad_query, grad_set = attend_layer(
        weights, encoded_all, queries[0], pos_bias[0], nbr_ids[0], ctx_grad[0]
    )
    section_count = lax.axis_size("section")
    kv_grad = lax.psum_scatter(
        lax.dot_general(
            grad_set, encoded_all, (((0,), (0,)), ((), ())), preferred_element_type=jnp.float32
        ).astype(jnp.bfloat16),
        "dp",
        scatter_dimension=0,
        tiled=True,
    ).astype(jnp.float32)
    grad_encoded = jnp.dot(grad_set, weights, preferred_element_type=jnp.float32).reshape(
        NSET, NLEN, ENC_D
    )
    state_grads = lax.psum_scatter(
        grad_encoded.astype(jnp.bfloat16), "section", scatter_dimension=1, tiled=True
    ).astype(jnp.float32)
    grad_flat = state_grads.reshape(-1, ENC_D)
    gain_part = jnp.sum(grad_flat * normed, axis=0)
    grad_normed = grad_flat * enc_gain[None, :]
    grad_mixed = inverse * (
        grad_normed - normed * jnp.mean(grad_normed * normed, axis=-1, keepdims=True)
    )
    grad_low = grad_mixed.astype(jnp.bfloat16)
    embed_grad = grad_mixed + lax.dot_general(
        grad_low, enc_weight, (((1,), (1,)), ((), ())), preferred_element_type=jnp.float32
    )
    embed_grad = embed_grad.astype(jnp.bfloat16).reshape(nbr_embed.shape)
    weight_part = lax.dot_general(
        local_rows, grad_low, (((0,), (0,)), ((), ())), preferred_element_type=jnp.float32
    )
    rows_here = ENC_D // section_count
    weight_total, gain_grad = lax.psum((weight_part, gain_part), ("section", "dp"))
    enc_grad = lax.dynamic_slice_in_dim(
        weight_total, lax.axis_index("section") * rows_here, rows_here, 0
    )
    return (grad_query[None], kv_grad[None], enc_grad, gain_grad, embed_grad)


def solution(mesh):
    return jax.shard_map(
        body,
        mesh=mesh,
        in_specs=(
            P("dp", None, "section", None),
            P(),
            P(),
            P("section", None, None),
            P("section", "dp", None),
            P("section", None, None, None),
            P("dp", None, None),
            P("section", "dp", None),
        ),
        out_specs=(
            P("section", "dp", None),
            P("section", "dp", None),
            P("section", None),
            P(),
            P("dp", None, "section", None),
        ),
        check_vma=False,
    )
```

profile of v0, /device:TPU:1, one launch (start us, length us, event | category | flops | bytes accessed | tf_op | source)
XLA Modules:
  0.0 480.3 jit_solution(3166054484189631501)
XLA Ops:
  8.0 0.0 reduce-scatter.5.cloned.1.call-start
  8.1 1.3 copy-done
  9.4 1.4 multiply_reduce_fusion
  10.9 0.1 copy.45
  11.0 0.9 copy.46
  11.9 0.1 multiply_convert_fusion
  12.0 26.1 %all_gather.3 = bf16[4,128,896]{2,1,0:T(8,128)(2,1)S(1)} all-gather(bf16[4,16,896]{2,1,0:T(8,128)(2,1)S(1)} %bitcast.111), channel_id=1, replica_groups=mesh['section'=8,'dp'=32] {'section'}, dimensions={1}, use_global_device_ids=true | all-gather | bytes 1032192 | tf_op jit(solution)/shard_map/all_gather | solution.py:89
  38.1 0.1 bitcast_convert_fusion.2
  38.2 9.6 %fusion.11 = bf16[512,4096]{1,0:T(8,128)(2,1)} fusion(bf16[512,896]{1,0:T(8,128)(2,1)S(1)} %bitcast.104, bf16[1,4096,896]{2,1,0:T(8,128)(2,1)} %param.11), kind=kOutput, calls=%fused_computation.11 | convolution fusion | flops 3760193536 | bytes 12451840 | tf_op jit(solution)/shard_map/dot_general | solution.py:26
  47.8 11.1 %convolution_convert_fusion = bf16[2,2,128,4096]{3,1,2,0:T(2,128)(2,1)} fusion(bf16[4,128,4096]{2,1,0:T(8,128)(2,1)} %bitcast.117, s32[2,2]{1,0:T(2,128)S(1)} %bitcast.115), kind=kOutput, calls=%fused_computation.12 | convolution fusion | flops 18874384 | bytes 8388624 | tf_op jit(solution)/shard_map/cne,eld->cnld/dot_general | solution.py:33
  59.0 5.1 %copy.22 = bf16[2,2,128,4096]{3,2,1,0:T(8,128)(2,1)S(1)} copy(bf16[2,2,128,4096]{3,1,2,0:T(2,128)(2,1)} %convolution_convert_fusion) | data formatting | bytes 8388608 | tf_op jit(solution)/shard_map/convert_element_type | solution.py:35
  64.1 2.3 fusion.52
  66.4 4.0 copy.26
  70.3 4.1 copy.23
  74.4 2.0 fusion.37
  76.5 2.0 fusion.53
  78.5 7.4 %convolution_bitcast_fusion = bf16[2,256,16,128]{3,1,2,0:T(8,128)(2,1)} fusion(bf16[2,64,16,128]{3,2,1,0:T(8,128)(2,1)} %bitcast.107, f32[2,16,64]{2,1,0:T(8,128)S(1)} %get-tuple-element.21, f32[2,16,256,64]{2,3,1,0:T(8,128)} %copy-done.2, f32[16,64,256]{2,1,0:T(8,128)S(1)} %bitcast_convert_fusion.2), kind=kOutput, calls=%fused_computation.18 | convolution fusion | flops 136841472 | bytes 5775360 | tf_op jit(solution)/shard_map/chqk,cqhd->ckhd/dot_general | solution.py:64
  85.8 4.3 copy.34
  90.1 4.2 concatenate.9
  94.3 5.3 %copy.36 = bf16[2,2,128,2048]{3,1,0,2:T(2,128)(2,1)} copy(bf16[2,2,128,2048]{3,2,1,0:T(8,128)(2,1)} %concatenate.9) | data formatting | bytes 4194304 | tf_op jit(solution)/shard_map/concatenate | solution.py:67
  99.6 0.9 fusion.18
  100.6 0.7 fusion.20
  101.3 0.9 multiply_bitcast_fusion
  102.2 2.7 copy.32
  104.9 4.6 concatenate.8
  109.5 3.9 copy.35
  113.4 8.1 %bitcast_convert_fusion.1 = bf16[4,128,4096]{2,0,1:T(4,128)(2,1)S(1)} fusion(bf16[2,2,128,2048]{3,1,0,2:T(2,128)(2,1)S(1)} %copy-done.4, bf16[2,2,128,2048]{3,1,0,2:T(2,128)(2,1)S(1)} %copy.35, s32[2,2]{1,0:T(2,128)S(1)} %bitcast.116), kind=kOutput, calls=%fused_computation.6 | convolution fusion | flops 25165840 | bytes 8388624 | tf_op jit(solution)/shard_map/cne,cnld->eld/dot_general | solution.py:75
  121.6 2.1 copy-done.13
  123.6 8.3 %fusion.22 = bf16[4,128,896]{2,1,0:T(8,128)(2,1)} fusion(bf16[1,4096,896]{2,1,0:T(8,128)(2,1)S(1)} %bitcast.114, bf16[4,128,4096]{2,0,1:T(4,128)(2,1)S(1)} %bitcast_convert_fusion.1), kind=kOutput, calls=%fused_computation.28 | convolution fusion | flops 3758555136 | bytes 12451840 | tf_op jit(solution)/shard_map/dot_general | solution.py:105
  132.0 0.0 reduce-scatter.5.cloned.1.call-update
  132.0 0.0 all-reduce.2.cloned.1.call-start
  132.0 44.1 %reduce-scatter.5.cloned.1.call-done = bf16[4,16,896]{2,1,0:T(8,128)(2,1)} async-done(((bf16[4,128,896]{2,1,0:T(8,128)(2,1)}), bf16[4,16,896]{2,1,0:T(8,128)(2,1)}) %reduce-scatter.5.cloned.1.call-update) | async-done | bytes 114704 | tf_op jit(solution)/shard_map/reduce_scatter | solution.py:108
  176.1 1.1 fusion.43
  177.2 1.0 fusion.42
  178.3 2.3 convolution_bitcast_fusion.1
  180.5 0.0 all-reduce.2.cloned.1.call-update
  180.5 0.2 reduce-scatter.3.cloned.1.call-start
  180.8 12.9 %bitcast_convert_fusion = bf16[4096,896]{1,0:T(8,128)(2,1)} fusion(bf16[4,128,896]{2,1,0:T(8,128)(2,1)} %copy-done.5, bf16[4,128,4096]{2,0,1:T(4,128)(2,1)} %copy-done.13), kind=kOutput, calls=%fused_computation.1 | convolution fusion | flops 3761766400 | bytes 12451840 | tf_op jit(solution)/shard_map/dot_general | solution.py:98
  193.6 0.0 reduce-scatter.3.cloned.1.call-update
  193.7 2.4 fusion.28
  196.1 0.3 copy.30
  196.5 1.0 broadcast_in_dim_reshape.3
  197.5 92.7 %psum.15 = f32[896]{0:T(1024)} all-reduce(f32[896]{0:T(1024)S(1)} %get-tuple-element.15), channel_id=1, replica_groups=mesh['section'=8,'dp'=32] {'section','dp'}, use_global_device_ids=true, to_apply=%region_9.0 | all-reduce | flops 896 | bytes 7168 | tf_op jit(solution)/shard_map/psum | solution.py:126
  290.1 1.3 fusion.29
  291.4 177.2 %all-reduce.2.cloned.1.call-done = f32[896,896]{0,1:T(8,128)} async-done(((f32[896,896]{0,1:T(8,128)}), f32[896,896]{0,1:T(8,128)}) %all-reduce.2.cloned.1.call-update) | async-done | bytes 3211280 | tf_op jit(solution)/shard_map/psum | solution.py:126
  468.6 1.4 constant_dynamic-slice_fusion
  469.9 0.9 copy.39
  470.9 1.7 bitcast_convert_fusion.3
  (34 shorter events, 0.1 us)
Async XLA Ops:
  8.0 1.4 copy-start
  8.0 2.9 copy-start.7
  8.0 3.0 copy-start.8
  8.0 3.9 copy-start.11
  8.0 168.1 %reduce-scatter.5.cloned.1.call-start = ((), (), s32[]{:S(2)}) async-start(), calls=%async_computation.3 | async-start | bytes 1032192 | tf_op jit(solution)/shard_map/reduce_scatter | solution.py:108
  10.9 27.2 %copy-start.6 = (bf16[1,16,64,256]{3,2,1,0:T(8,128)(2,1)S(1)}, bf16[1,16,64,256]{3,2,1,0:T(8,128)(2,1)}, u32[]{:S(2)}) copy-start(bf16[1,16,64,256]{3,2,1,0:T(8,128)(2,1)} %param.13) | copy-start | bytes 1572868
  38.1 9.7 %copy-start.5 = (bf16[4,128,896]{2,1,0:T(8,128)(2,1)}, bf16[4,128,896]{2,1,0:T(8,128)(2,1)S(1)}, u32[]{:S(2)}) copy-start(bf16[4,128,896]{2,1,0:T(8,128)(2,1)S(1)} %all_gather.3) | copy-start | bytes 2752516
  38.2 9.6 %copy-start.12 = (s32[1,2,2]{2,1,0:T(2,128)S(1)}, s32[1,2,2]{2,1,0:T(2,128)}, u32[]{:S(2)}) copy-start(s32[1,2,2]{2,1,0:T(2,128)} %param.14) | copy-start | bytes 52
  76.5 2.0 copy-start.2
  90.1 9.5 %copy-start.9 = (bf16[16,8,16,128]{3,2,1,0:T(8,128)(2,1)S(1)}, bf16[16,8,16,128]{3,2,1,0:T(8,128)(2,1)}, u32[]{:S(2)}) copy-start(bf16[16,8,16,128]{3,2,1,0:T(8,128)(2,1)} %copy.46) | copy-start | bytes 1572868
  94.3 5.3 %copy-start.1 = (f32[2,16,64,256]{3,2,1,0:T(8,128)S(1)}, f32[2,16,64,256]{3,2,1,0:T(8,128)}, u32[]{:S(2)}) copy-start(f32[2,16,64,256]{3,2,1,0:T(8,128)} %get-tuple-element.22) | copy-start | bytes 6291460
  94.3 5.3 %copy-start.3 = (bf16[2,256,2048]{1,2,0:T(8,128)(2,1)S(1)}, bf16[2,256,2048]{1,2,0:T(8,128)(2,1)}, u32[]{:S(2)}) copy-start(bf16[2,256,2048]{1,2,0:T(8,128)(2,1)} %copy.26) | copy-start | bytes 6291460
  109.4 4.0 copy-start.4
  109.4 14.2 %slice-start = ((s8[7340032]{0:T(1024)(128)(4,1)}), s8[4194304]{0:T(1024)(128)(4,1)S(1)}, s32[]{:S(2)}) async-start(s8[7340032]{0:T(1024)(128)(4,1)} %bitcast.113), calls=%async_computation.5 | async-start | bytes 8388608
  113.4 10.2 %slice-start.1 = ((s8[7340032]{0:T(1024)(128)(4,1)}), s8[3145728]{0:T(1024)(128)(4,1)S(1)}, s32[]{:S(2)}) async-start(s8[7340032]{0:T(1024)(128)(4,1)} %bitcast.113), calls=%async_computation.6 | async-start | bytes 6291456
  121.5 2.1 copy-start.13
  123.6 54.6 %copy-start.10 = (bf16[1,4,16,896]{3,2,1,0:T(8,128)(2,1)S(1)}, bf16[1,4,16,896]{3,2,1,0:T(8,128)(2,1)}, u32[]{:S(2)}) copy-start(bf16[1,4,16,896]{3,2,1,0:T(8,128)(2,1)} %param.8) | copy-start | bytes 344068
  132.0 336.6 %all-reduce.2.cloned.1.call-start = ((), (), s32[]{:S(2)}) async-start(), calls=%async_computation.4 | async-start | bytes 6422528 | tf_op jit(solution)/shard_map/psum | solution.py:126
  180.5 290.3 %reduce-scatter.3.cloned.1.call-start = ((), (), s32[]{:S(2)}) async-start(), calls=%async_computation.2 | async-start | bytes 7569408 | tf_op jit(solution)/shard_map/reduce_scatter | solution.py:97
Sparse Core Ops, SparseCore 0:
  132.1 43.9 reduce-scatter.4
  181.6 286.9 all-reduce.1
Sparse Core Ops, SparseCore 1:
  193.8 141.9 reduce-scatter.2
where the time goes:
time: 485 us; the launch traced here: 480 us
  waiting for transfers between devices  221 us (46%)
  blocking collectives  119 us (25%)
  matrix products  68.6 us (14%)
  local copies, waits for them, and re-layouts  48.6 us (10%)
  between operations  16 us (3%)
  other arithmetic  6.78 us (1%)
    psum x1, waiting for transfers between devices, body(): lax.psum((weight_part, gain_part), ('section', 'dp'))  177 us
    psum x1, blocking collectives, body(): lax.psum((weight_part, gain_part), ('section', 'dp'))  92.7 us
    reduce_scatter x1, waiting for transfers between devices, body(): lax.psum_scatter(grad_encoded.astype(jnp.bfloat16), 'section', scatter_di...  44.1 us
    all_gather x1, blocking collectives, body(): lax.all_gather(encoded_local, 'section', axis=1, tiled=True)  26.1 us
    concatenate x4, local copies, waits for them, and re-layouts, attend_layer(): jnp.concatenate([grad_keys.reshape(blocks, key_rows, head_width), grad_va...  18 us
    dot_general x1, matrix products, body(): lax.dot_general(grad_set, encoded_all, (((0,), (0,)), ((), ())), preferre...  12.9 us
    dot_general x1, matrix products, attend_layer(): jnp.einsum('cne,eld->cnld', selector, projected, preferred_element_type=j...  11.1 us
  transfers between devices with their start and end apart: 3, of which 2 were waited for; matrix products, arithmetic and copies ran while one was open for 4% of the time, Pallas kernels for 0%

commit v1 on v0

v1 whole, which is shorter than its diff:
```python
import math

import jax
import jax.numpy as jnp
from jax import lax
from jax.experimental import pallas as pl
from jax.experimental.pallas import tpu as pltpu
from jax.sharding import PartitionSpec as P

HEADS = 16
HEAD = 128
ENC_D = 896
BLOCK = 64
NBR = 2
NLEN = 128
TOK_DEV = 128
NSET = 4
ROWS = NSET * NLEN
N_SEC = 8
N_Z = 8
LOCAL = NLEN // N_SEC
OWN_ROWS = ENC_D // N_SEC
PIECE = 16
QUAD_COLS = 256
FACTOR = 1.0 / math.sqrt(HEAD)
MESH = pl.DeviceIdType.MESH

eps_norm = 1e-06

VMEM_SPEC = pl.BlockSpec(memory_space=pltpu.VMEM)


def greet(peers):
    barrier = pltpu.get_barrier_semaphore()
    for peer in peers:
        pl.semaphore_signal(barrier, inc=1, device_id=peer, device_id_type=MESH)
    pl.semaphore_wait(barrier, len(peers))


def remote(src, dst, send_sem, recv_sem, peer):
    return pltpu.make_async_remote_copy(
        src_ref=src,
        dst_ref=dst,
        send_sem=send_sem,
        recv_sem=recv_sem,
        device_id=peer,
        device_id_type=MESH,
    )


def section_ids(me):
    y, x = me // 4, lax.rem(me, 4)
    steps = [(1, 0), (0, 1), (0, 3), (1, 1), (1, 3), (0, 2), (1, 2)]
    return [lax.rem(y + a, 2) * 4 + lax.rem(x + b, 4) for a, b in steps]


def section_sources(me):
    y, x = me // 4, lax.rem(me, 4)
    steps = [(1, 0), (0, 3), (0, 1), (1, 3), (1, 1), (0, 2), (1, 2)]
    return [lax.rem(y + a, 2) * 4 + lax.rem(x + b, 4) for a, b in steps]


def row_slot(index):
    return pl.ds(pl.multiple_of(index * LOCAL, LOCAL), LOCAL)


def dot_nt(a, b):
    return lax.dot_general(a, b, (((1,), (1,)), ((), ())), preferred_element_type=jnp.float32)


def dot_tn(a, b):
    return lax.dot_general(a, b, (((0,), (0,)), ((), ())), preferred_element_type=jnp.float32)


def dot_nn(a, b):
    return jnp.dot(a, b, preferred_element_type=jnp.float32)


def encode(x, enc_weight):
    mixed = x.astype(jnp.float32) + dot_nn(x, enc_weight)
    inverse = lax.rsqrt(jnp.mean(mixed * mixed, axis=-1, keepdims=True) + eps_norm)
    return mixed * inverse, inverse


def f32(x):
    return x.astype(jnp.float32)


def low(x):
    return x.astype(jnp.bfloat16)


def train_kernel(
    ids_ref,
    x_ref,
    gain_ref,
    encw_hbm,
    w_hbm,
    q_hbm,
    bias_hbm,
    g_hbm,
    qg_ref,
    kvg_ref,
    wg_ref,
    gg_ref,
    eg_ref,
    encw_ref,
    w_ref,
    q_ref,
    bias_ref,
    g_ref,
    x_all,
    enc_ref,
    xt_ref,
    gs_ref,
    dw_ref,
    core_recv,
    first_ref,
    plus_recv,
    minus_recv,
    fin_ref,
    y_recv,
    de_ref,
    de_recv,
    low_all,
    low_loc,
    gain_all,
    gain_loc,
    wp_ref,
    quad_recv,
    zp_ref,
    z_recv,
    za_ref,
    za_all,
    wa_all,
    load_sem,
    x_send,
    x_rsem,
    core_send,
    core_rsem,
    ring_send,
    ring_rsem,
    y_send,
    y_rsem,
    sec_send,
    sec_rsem,
    low_send,
    low_rsem,
    gn_send,
    gn_rsem,
    quad_send,
    quad_rsem,
    z_send,
    z_rsem,
    za_send,
    za_rsem,
    wa_send,
    wa_rsem,
):
    me = lax.axis_index("section")
    dp = lax.axis_index("dp")
    core = lax.rem(dp, 2)
    zed = lax.rem(dp // 2, N_Z)
    yhi = dp // (2 * N_Z)

    loads = [
        pltpu.make_async_copy(encw_hbm, encw_ref, load_sem.at[0]),
        pltpu.make_async_copy(w_hbm.at[0], w_ref, load_sem.at[1]),
        pltpu.make_async_copy(q_hbm.at[0], q_ref, load_sem.at[2]),
        pltpu.make_async_copy(bias_hbm.at[0], bias_ref, load_sem.at[3]),
        pltpu.make_async_copy(g_hbm.at[0], g_ref, load_sem.at[4]),
    ]
    for copy in loads:
        copy.start()

    def dp_peer(y, z, c):
        return {"dp": (y * N_Z + z) * 2 + c}

    targets = section_ids(me)
    sources = section_sources(me)
    sec = [{"section": t} for t in targets]
    z_peers = [dp_peer(yhi, lax.rem(zed + d, N_Z), core) for d in range(1, N_Z)]
    z_next, z_prev = z_peers[0], z_peers[N_Z - 2]
    core_peer = dp_peer(yhi, zed, 1 - core)
    y_peer = dp_peer(1 - yhi, zed, core)
    quad = [core_peer, y_peer, dp_peer(1 - yhi, zed, 1 - core)]
    greet(sec + z_peers + quad)

    x_copies = []
    for i, peer in enumerate(sec):
        copy = remote(x_ref, x_all.at[:, row_slot(me), :], x_send.at[i], x_rsem.at[i], peer)
        copy.start()
        x_copies.append(copy)
    x_all[:, row_slot(me), :] = x_ref[...]
    loads[0].wait()

    def encode_slots(slots):
        x = jnp.concatenate(
            [x_all[:, row_slot(s), :].reshape(NSET * LOCAL, ENC_D) for s in slots], axis=0
        )
        normed, _ = encode(x, encw_ref[...])
        encoded = low(normed * gain_ref[...])
        for n, s in enumerate(slots):
            enc_ref[:, row_slot(s), :] = encoded[
                n * NSET * LOCAL : (n + 1) * NSET * LOCAL
            ].reshape(NSET, LOCAL, ENC_D)

    for i in range(3):
        x_copies[i].wait_recv()
    encode_slots([me] + sources[:3])
    for i in range(3, 7):
        x_copies[i].wait_recv()
    encode_slots(sources[3:])
    for copy in loads[1:]:
        copy.wait()

    def picked(n, parts):
        chosen = parts[NSET - 1]
        for e in range(NSET - 2, -1, -1):
            chosen = jnp.where(ids_ref[n : n + 1, :] == e, parts[e], chosen)
        return chosen

    def core_z(i):
        half = (i + 1) // 2
        return lax.rem(zed + 4 + half * (1 - 2 * lax.rem(i, 2)), N_Z)

    def core_copy(i):
        z = core_z(i)
        return remote(
            dw_ref.at[1 - core, z], core_recv.at[z], core_send.at[i], core_rsem.at[i], core_peer
        )

    def chip_sum(z, y):
        return f32(dw_ref[core, z, y]) + f32(core_recv[z, y])

    def ring_copies(s):
        if s == 0:
            pairs = (
                (first_ref.at[0], plus_recv.at[0, 0], z_next),
                (first_ref.at[1], minus_recv.at[0, 1], z_prev),
            )
        else:
            pairs = (
                (plus_recv.at[s - 1], plus_recv.at[s], z_next),
                (minus_recv.at[s - 1], minus_recv.at[s], z_prev),
            )
        return [
            remote(src, dst, ring_send.at[s, n], ring_rsem.at[s, n], peer)
            for n, (src, dst, peer) in enumerate(pairs)
        ]

    def ring_step(s):
        zp = lax.rem(zed + 4 - s, N_Z)
        zm = lax.rem(zed + 4 + s, N_Z)
        copies = ring_copies(s)
        if s == 0:
            core_copy(0).wait_recv()
            for y in range(2):
                first_ref[y] = low(chip_sum(zp, y))
                copies[y].start()
            return
        earlier = ring_copies(s - 1)
        core_copy(2 * s - 1).wait_recv()
        earlier[0].wait_recv()
        for y in range(2):
            value = chip_sum(zp, y)
            if s > 1 or y == 0:
                value = value + f32(plus_recv[s - 1, y])
            plus_recv[s - 1, y] = low(value)
        copies[0].start()
        core_copy(2 * s).wait_recv()
        earlier[1].wait_recv()
        for y in range(2):
            value = chip_sum(zm, y)
            if s > 1 or y == 1:
                value = value + f32(minus_recv[s - 1, y])
            minus_recv[s - 1, y] = low(value)
        copies[1].start()

    def pair(i, carry):
        z = core_z(i)
        cols = pl.ds(pl.multiple_of(z * 2 * HEAD, 2 * HEAD), 2 * HEAD)
        vcols = pl.ds(
            pl.multiple_of(HEADS * HEAD + z * 2 * HEAD, 2 * HEAD), 2 * HEAD
        )
        enc = enc_ref[...].reshape(ROWS, ENC_D)
        keys = low(dot_nt(enc, w_ref[cols, :]))
        vals = low(dot_nt(enc, w_ref[vcols, :]))
        q2, g2 = q_ref[:, cols], g_ref[:, cols]
        dks, dvs, dkts, dvts, dqs = [], [], [], [], []
        heads = []
        for a in range(2):
            span = slice(a * HEAD, (a + 1) * HEAD)
            s_all = dot_nt(keys[:, span], q2[:, span])
            dp_all = dot_nt(vals[:, span], g2[:, span])
            b = f32(bias_ref[2 * z + a])
            heads.append((jnp.concatenate([b, b], axis=0).T, span, s_all, dp_all))
        for bias, span, s_all, dp_all in heads:
            q, g, k = q2[:, span], g2[:, span], keys[:, span]
            s_sets = [s_all[e * NLEN : (e + 1) * NLEN] for e in range(NSET)]
            dp_sets = [dp_all[e * NLEN : (e + 1) * NLEN] for e in range(NSET)]
            scores = [
                picked(n, s_sets) * FACTOR + bias[n * NLEN : (n + 1) * NLEN]
                for n in range(NBR)
            ]
            dprobs = [picked(n, dp_sets) for n in range(NBR)]
            peak = jnp.max(jnp.maximum(scores[0], scores[1]), axis=0, keepdims=True)
            ex = [jnp.exp(s - peak) for s in scores]
            share = 1.0 / jnp.sum(ex[0] + ex[1], axis=0, keepdims=True)
            p = [e * share for e in ex]
            inner = jnp.sum(p[0] * dprobs[0] + p[1] * dprobs[1], axis=0, keepdims=True)
            ds = [f32(low(p[n] * (dprobs[n] - inner))) for n in range(NBR)]
            pb = [f32(low(p[n])) for n in range(NBR)]
            zero = jnp.zeros_like(ds[0])
            ds_t, p_t = [], []
            for e in range(NSET):
                hit = [ids_ref[n : n + 1, :] == e for n in range(NBR)]
                ds_t.append(low(jnp.where(hit[0], ds[0], zero) + jnp.where(hit[1], ds[1], zero)))
                p_t.append(low(jnp.where(hit[0], pb[0], zero) + jnp.where(hit[1], pb[1], zero)))
            ds_t = jnp.concatenate(ds_t, axis=0)
            p_t = jnp.concatenate(p_t, axis=0)
            dks.append(low(dot_nn(ds_t, q) * FACTOR))
            dvs.append(low(dot_nn(p_t, g)))
            dkts.append(low(dot_nt(q.T, ds_t) * FACTOR))
            dvts.append(low(dot_nt(g.T, p_t)))
            dqs.append(low(dot_tn(ds_t, k) * FACTOR))
        qg_ref[0, :, cols] = jnp.concatenate(dqs, axis=1)
        gs_ref[:, cols] = jnp.concatenate(dks, axis=1)
        gs_ref[:, vcols] = jnp.concatenate(dvs, axis=1)
        dw = low(dot_nn(jnp.concatenate(dkts + dvts, axis=0), enc))
        for y in range(2):
            for c in range(2):
                at = (2 * y + c) * HEAD
                dw_ref[c, z, y] = dw[at : at + HEAD]
        core_copy(i).start()
        for s in range(4):

            @pl.when(i == 2 * s + 1)
            def _(s=s):
                ring_step(s)

        return carry

    lax.fori_loop(0, N_Z, pair, 0)

    sec_copies = []
    for half in range(2):
        rows = pl.ds(half * 2 * NLEN, 2 * NLEN)
        de_ref[2 * half : 2 * half + 2] = low(dot_nn(gs_ref[rows, :], w_ref[...])).reshape(
            2, NLEN, ENC_D
        )
        for i, peer in enumerate(sec):
            copy = remote(
                de_ref.at[2 * half : 2 * half + 2, row_slot(targets[i]), :],
                de_recv.at[i, 2 * half : 2 * half + 2],
                sec_send.at[half, i],
                sec_rsem.at[half, i],
                peer,
            )
            copy.start()
            sec_copies.append(copy)

    normed, inverse = encode(x_ref[...].reshape(NSET * LOCAL, ENC_D), encw_ref[...])
    xt_ref[...] = x_all[...].reshape(ROWS, ENC_D).T

    core_copy(N_Z - 1).wait_recv()
    for copy in ring_copies(3):
        copy.wait_recv()
    for y in range(2):
        fin_ref[y] = low(chip_sum(zed, y) + f32(plus_recv[3, y]) + f32(minus_recv[3, y]))
    y_copy = remote(fin_ref.at[1 - yhi], y_recv, y_send, y_rsem, y_peer)
    y_copy.start()

    for copy in sec_copies:
        copy.wait_recv()
    grad = f32(de_ref[:, row_slot(me), :])
    for i in range(N_SEC - 1):
        grad = grad + f32(de_recv[i])
    grad = grad.reshape(NSET * LOCAL, ENC_D)
    grad_normed = grad * gain_ref[...]
    grad_mixed = inverse * (
        grad_normed - normed * jnp.mean(grad_normed * normed, axis=-1, keepdims=True)
    )
    grad_low = low(grad_mixed)
    low_loc[...] = grad_low.reshape(NSET, LOCAL, ENC_D)
    low_copies = []
    for i, peer in enumerate(sec):
        copy = remote(
            low_loc, low_all.at[:, row_slot(me), :], low_send.at[i], low_rsem.at[i], peer
        )
        copy.start()
        low_copies.append(copy)
    gain_row = jnp.sum(grad * normed, axis=0, keepdims=True)
    gain_loc[...] = jnp.concatenate(
        [gain_row[:, i * 128 : (i + 1) * 128] for i in range(7)]
        + [jnp.zeros((1, 128), jnp.float32)],
        axis=0,
    )
    for i, peer in enumerate(sec):
        copy = remote(gain_loc, gain_all.at[i], gn_send.at[i], gn_rsem.at[i], peer)
        copy.start()
        low_copies.append(copy)
    low_all[:, row_slot(me), :] = low_loc[...]
    embed = grad_mixed + dot_nt(grad_low, encw_ref[...])
    eg_ref[...] = low(embed).reshape(NSET, LOCAL, ENC_D)

    y_copy.wait_recv()
    kvg_ref[...] = f32(fin_ref[yhi]) + f32(y_recv[...])

    for copy in low_copies:
        copy.wait_recv()
    weight = dot_nn(
        xt_ref[pl.ds(pl.multiple_of(me * OWN_ROWS, 16), OWN_ROWS), :],
        low_all[...].reshape(ROWS, ENC_D),
    )
    gain_sum = gain_loc[...]
    for i in range(N_SEC - 1):
        gain_sum = gain_sum + gain_all[i]
    weight = jnp.concatenate([weight, jnp.zeros((OWN_ROWS, 128), jnp.float32)], axis=1)
    for j in range(4):
        wp_ref[j, 0 : N_Z - 1] = low(weight[:, j * QUAD_COLS : (j + 1) * QUAD_COLS]).reshape(
            N_Z - 1, PIECE, QUAD_COLS
        )
        extra = jnp.zeros((PIECE, QUAD_COLS), jnp.float32)
        if j == 0:
            extra = jnp.concatenate(
                [
                    jnp.concatenate([gain_sum, jnp.zeros((8, 128), jnp.float32)], axis=1),
                    jnp.zeros((8, QUAD_COLS), jnp.float32),
                ],
                axis=0,
            )
        wp_ref[j, N_Z - 1] = low(extra)
    my_quad = yhi * 2 + core
    quad_ids = [yhi * 2 + (1 - core), (1 - yhi) * 2 + core, (1 - yhi) * 2 + (1 - core)]
    quad_copies = []
    for i in range(3):
        copy = remote(
            wp_ref.at[quad_ids[i]], quad_recv.at[i], quad_send.at[i], quad_rsem.at[i], quad[i]
        )
        copy.start()
        quad_copies.append(copy)
    for copy in quad_copies:
        copy.wait_recv()
    zp_ref[...] = low(
        f32(wp_ref[my_quad]) + f32(quad_recv[0]) + f32(quad_recv[1]) + f32(quad_recv[2])
    )
    z_copies = []
    for i, peer in enumerate(z_peers):
        copy = remote(
            zp_ref.at[lax.rem(zed + i + 1, N_Z)], z_recv.at[i], z_send.at[i], z_rsem.at[i], peer
        )
        copy.start()
        z_copies.append(copy)
    total = f32(zp_ref[zed])
    for i in range(N_Z - 1):
        z_copies[i].wait_recv()
        total = total + f32(z_recv[i])
    za_ref[...] = low(total)
    za_copies = []
    for i, peer in enumerate(z_peers):
        copy = remote(za_ref, za_all.at[zed], za_send.at[i], za_rsem.at[i], peer)
        copy.start()
        za_copies.append(copy)
    za_all[zed] = za_ref[...]
    for copy in za_copies:
        copy.wait_recv()
    wa_copies = []
    for i in range(3):
        copy = remote(za_all, wa_all.at[my_quad], wa_send.at[i], wa_rsem.at[i], quad[i])
        copy.start()
        wa_copies.append(copy)
    wa_all[my_quad] = za_all[...]

    y_copy.wait_send()
    for group in (x_copies, sec_copies, low_copies, quad_copies, z_copies, za_copies):
        for copy in group:
            copy.wait_send()
    for i in range(N_Z):
        core_copy(i).wait_send()
    for s in range(4):
        for copy in ring_copies(s):
            copy.wait_send()

    for copy in wa_copies:
        copy.wait_recv()
    for j in range(4):
        width = min(QUAD_COLS, ENC_D - j * QUAD_COLS)
        wg_ref[:, j * QUAD_COLS : j * QUAD_COLS + width] = f32(
            wa_all[j, 0 : N_Z - 1].reshape(OWN_ROWS, QUAD_COLS)[:, :width]
        )
    gg_ref[...] = f32(wa_all[0, N_Z - 1])[:8, :128]
    for copy in wa_copies:
        copy.wait_send()


def train(ids, x_local, gain, enc_weight, kv_weight, queries, pos_bias, ctx_grad):
    bf, fl = jnp.bfloat16, jnp.float32
    dma = pltpu.SemaphoreType.DMA
    vmem = pltpu.VMEM
    any_spec = pl.BlockSpec(memory_space=pl.ANY)
    width = HEADS * HEAD
    return pl.pallas_call(
        train_kernel,
        out_shape=[
            jax.ShapeDtypeStruct((1, TOK_DEV, width), bf),
            jax.ShapeDtypeStruct((HEAD, ENC_D), fl),
            jax.ShapeDtypeStruct((OWN_ROWS, ENC_D), fl),
            jax.ShapeDtypeStruct((8, 128), fl),
            jax.ShapeDtypeStruct((NSET, LOCAL, ENC_D), bf),
        ],
        in_specs=[VMEM_SPEC] * 3 + [any_spec] * 5,
        out_specs=[VMEM_SPEC] * 5,
        scratch_shapes=[
            vmem((ENC_D, ENC_D), bf),
            vmem((2 * width, ENC_D), bf),
            vmem((TOK_DEV, width), bf),
            vmem((HEADS, BLOCK, NBR * NLEN), bf),
            vmem((TOK_DEV, width), bf),
            vmem((NSET, NLEN, ENC_D), bf),
            vmem((NSET, NLEN, ENC_D), bf),
            vmem((ENC_D, ROWS), bf),
            vmem((ROWS, 2 * width), bf),
            vmem((2, N_Z, 2, HEAD, ENC_D), bf),
            vmem((N_Z, 2, HEAD, ENC_D), bf),
            vmem((2, HEAD, ENC_D), bf),
            vmem((4, 2, HEAD, ENC_D), bf),
            vmem((4, 2, HEAD, ENC_D), bf),
            vmem((2, HEAD, ENC_D), bf),
            vmem((HEAD, ENC_D), bf),
            vmem((NSET, NLEN, ENC_D), bf),
            vmem((N_SEC - 1, NSET, LOCAL, ENC_D), bf),
            vmem((NSET, NLEN, ENC_D), bf),
            vmem((NSET, LOCAL, ENC_D), bf),
            vmem((N_SEC - 1, 8, 128), fl),
            vmem((8, 128), fl),
            vmem((4, N_Z, PIECE, QUAD_COLS), bf),
            vmem((3, N_Z, PIECE, QUAD_COLS), bf),
            vmem((N_Z, PIECE, QUAD_COLS), bf),
            vmem((N_Z - 1, PIECE, QUAD_COLS), bf),
            vmem((PIECE, QUAD_COLS), bf),
            vmem((N_Z, PIECE, QUAD_COLS), bf),
            vmem((4, N_Z, PIECE, QUAD_COLS), bf),
            dma((5,)),
            dma((7,)),
            dma((7,)),
            dma((8,)),
            dma((8,)),
            dma((4, 2)),
            dma((4, 2)),
            dma,
            dma,
            dma((2, 7)),
            dma((2, 7)),
            dma((7,)),
            dma((7,)),
            dma((7,)),
            dma((7,)),
            dma((3,)),
            dma((3,)),
            dma((7,)),
            dma((7,)),
            dma((7,)),
            dma((7,)),
            dma((3,)),
            dma((3,)),
        ],
        compiler_params=pltpu.CompilerParams(
            collective_id=0, has_side_effects=True, vmem_limit_bytes=62 * 1024 * 1024
        ),
        name="train",
    )(ids, x_local, gain, enc_weight, kv_weight, queries, pos_bias, ctx_grad)


def finish_kernel(q_in, k_in, w_in, g_in, e_in, q_out, k_out, w_out, g_out, e_out):
    q_out[...] = q_in[...]
    k_out[...] = k_in[...]
    w_out[...] = w_in[...]
    for i in range(7):
        g_out[:, i * 128 : (i + 1) * 128] = g_in[i : i + 1, :]
    e_out[...] = e_in[...]


def finish(outs):
    shapes = [jax.ShapeDtypeStruct(o.shape, o.dtype) for o in outs]
    shapes[3] = jax.ShapeDtypeStruct((1, ENC_D), jnp.float32)
    return pl.pallas_call(
        finish_kernel,
        out_shape=shapes,
        in_specs=[VMEM_SPEC] * 5,
        out_specs=[VMEM_SPEC] * 5,
        name="finish",
    )(*outs)


def body(nbr_embed, enc_weight, enc_gain, kv_weight, queries, pos_bias, nbr_ids, ctx_grad):
    outs = train(
        jnp.repeat(nbr_ids[0].T, BLOCK, axis=1),
        nbr_embed[0],
        enc_gain[None, :],
        enc_weight,
        kv_weight,
        queries,
        pos_bias,
        ctx_grad,
    )
    q_grad, kv_grad, w_grad, g_grad, e_grad = finish(outs)
    return (q_grad, kv_grad[None], w_grad, g_grad.reshape(ENC_D), e_grad[None])


def solution(mesh):
    return jax.shard_map(
        body,
        mesh=mesh,
        in_specs=(
            P("dp", None, "section", None),
            P(),
            P(),
            P("section", None, None),
            P("section", "dp", None),
            P("section", None, None, None),
            P("dp", None, None),
            P("section", "dp", None),
        ),
        out_specs=(
            P("section", "dp", None),
            P("section", "dp", None),
            P("section", None),
            P(),
            P("dp", None, "section", None),
        ),
        check_vma=False,
    )
```

time: 485 us -> 114 us (0.24)
  waiting for transfers between devices: 221 us -> 0 us
  blocking collectives: 119 us -> 0 us
  Pallas kernels: 0 us -> 109 us
  matrix products: 68.6 us -> 0 us
  local copies, waits for them, and re-layouts: 48.6 us -> 2.75 us
  between operations: 16 us -> 0.64 us
  other arithmetic: 6.78 us -> 1.27 us
    psum x1 -> x0, waiting for transfers between devices: 177 us -> none  [body(): lax.psum((weight_part, gain_part), ('section', 'dp'))]
    pallas_call x0 -> x2, Pallas kernels: none -> 109 us  [the longest x1 107 us: train(): pl.pallas_call(train_kernel, out_shape=[jax.ShapeDtypeStruct((1, TOK_DEV,...]
    psum x1 -> x0, blocking collectives: 92.7 us -> none  [body(): lax.psum((weight_part, gain_part), ('section', 'dp'))]
    dot_general x13 -> x0, matrix products: 68.6 us -> none  [the longest x1 12.9 us: body(): lax.dot_general(grad_set, encoded_all, (((0,), (0,)), ((), ())), preferre...]
    reduce_scatter x2 -> x0, waiting for transfers between devices: 44.1 us -> none  [the longest x1 44.1 us: body(): lax.psum_scatter(grad_encoded.astype(jnp.bfloat16), 'section', scatter_di...]
    all_gather x1 -> x0, blocking collectives: 26.1 us -> none  [body(): lax.all_gather(encoded_local, 'section', axis=1, tiled=True)]
    concatenate x4 -> x0, local copies, waits for them, and re-layouts: 18 us -> none  [attend_layer(): jnp.concatenate([grad_keys.reshape(blocks, key_rows, head_width), grad_va...]
    slice x3 -> x0, local copies, waits for them, and re-layouts: 10.4 us -> none  [the longest x2 6.25 us: attend_layer(): chosen[:, :, head_width:].reshape(blocks, key_rows, HEADS, HEAD)]
  transfers between devices with their start and end apart: 3 -> 0, of which waited for: 2 -> 0; matrix products, arithmetic and copies ran while one was open for 4% -> 0% of each run, Pallas kernels for 0% -> 0%
where the time goes in v1:
time: 114 us
  Pallas kernels  109 us (96%)
  local copies, waits for them, and re-layouts  2.75 us (2%)
  other arithmetic  1.27 us (1%)
    pallas_call x1, Pallas kernels, train(): pl.pallas_call(train_kernel, out_shape=[jax.ShapeDtypeStruct((1, TOK_DEV,...  107 us
    pallas_call x1, Pallas kernels, finish(): pl.pallas_call(finish_kernel, out_shape=shapes, in_specs=[VMEM_SPEC] * 5,...  2.46 us

profile of v1, /device:TPU:1, one launch (start us, length us, event | category | flops | bytes accessed | tf_op | source)
XLA Modules:
  0.0 113.9 jit_solution(13096756088244311857)
XLA Ops:
  0.6 0.8 copy.13
  1.4 0.1 broadcast_in_dim.12
  1.5 0.6 reshape.16.ids_ref
  2.1 1.3 %broadcast_in_dim.13.gain_ref = f32[1,896]{1,0:T(1,128)} reshape(f32[896]{0:T(1024)} %param.10) | data formatting | bytes 7168 | tf_op jit(solution)/shard_map/broadcast_in_dim | solution.py:600
  3.4 106.8 %train.1 = (bf16[1,128,2048]{2,1,0:T(8,128)(2,1)}, f32[128,896]{1,0:T(8,128)}, f32[112,896]{1,0:T(8,128)}, f32[8,128]{1,0:T(8,128)}, bf16[4,16,896]{2,1,0:T(8,128)(2,1)}) custom-call(s32[2,128]{1,0:T(2,128)} %reshape.16.ids_ref, bf16[4,16,896]{2,1,0:T(8,128)(2,1)} %bitcast.6, f32[1,896]{1,0:T(1,128)} %broadcast_in_dim.13.gain_ref, ...), custom_call_target="tpu_custom_call" | custom-call | tf_op jit(solution)/shard_map/train/pallas_call | solution.py:503
  110.2 2.5 %finish.1 = (bf16[1,128,2048]{2,1,0:T(8,128)(2,1)}, f32[128,896]{1,0:T(8,128)}, f32[112,896]{1,0:T(8,128)}, f32[1,896]{1,0:T(1,128)}, bf16[4,16,896]{2,1,0:T(8,128)(2,1)}) custom-call(bf16[1,128,2048]{2,1,0:T(8,128)(2,1)} %get-tuple-element.15.q_in, f32[128,896]{1,0:T(8,128)} %get-tuple-element.16.k_in, f32[112,896]{1,0:T(8,128)} %get-tuple-element.17.w_in, ...), custom_call_target="tpu_custom_call" | custom-call | tf_op jit(solution)/shard_map/finish/pallas_call | solution.py:587
  112.6 1.3 %reduce = f32[896]{0:T(1024)} reduce(f32[1,896]{1,0:T(1,128)} %get-tuple-element.23, f32[]{:T(128)} %constant.6), dimensions={0}, to_apply=%get-tuple-element.23.reduce_sub_computation | reduce | bytes 7172 | tf_op jit(solution)/shard_map/finish/pallas_call | solution.py:587

commit v2 on v1

--- a/solution.py
+++ b/solution.py
@@ -163,6 +163,7 @@
     zed = lax.rem(dp // 2, N_Z)
     yhi = dp // (2 * N_Z)
 
+    gain = gain_ref[...].reshape(1, ENC_D)
     loads = [
         pltpu.make_async_copy(encw_hbm, encw_ref, load_sem.at[0]),
         pltpu.make_async_copy(w_hbm.at[0], w_ref, load_sem.at[1]),
@@ -199,7 +200,7 @@
             [x_all[:, row_slot(s), :].reshape(NSET * LOCAL, ENC_D) for s in slots], axis=0
         )
         normed, _ = encode(x, encw_ref[...])
-        encoded = low(normed * gain_ref[...])
+        encoded = low(normed * gain)
         for n, s in enumerate(slots):
             enc_ref[:, row_slot(s), :] = encoded[
                 n * NSET * LOCAL : (n + 1) * NSET * LOCAL
@@ -214,10 +215,15 @@
     for copy in loads[1:]:
         copy.wait()
 
+    front = lax.broadcasted_iota(jnp.int32, (1, TOK_DEV), 1) < BLOCK
+    idm = ids_ref[0]
+    marks = [jnp.where(front, idm[0:1, n : n + 1], idm[1:2, n : n + 1]) for n in range(NBR)]
+    hits = [[marks[n] == e for e in range(NSET)] for n in range(NBR)]
+
     def picked(n, parts):
         chosen = parts[NSET - 1]
         for e in range(NSET - 2, -1, -1):
-            chosen = jnp.where(ids_ref[n : n + 1, :] == e, parts[e], chosen)
+            chosen = jnp.where(hits[n][e], parts[e], chosen)
         return chosen
 
     def core_z(i):
@@ -233,49 +239,33 @@
     def chip_sum(z, y):
         return f32(dw_ref[core, z, y]) + f32(core_recv[z, y])
 
-    def ring_copies(s):
-        if s == 0:
-            pairs = (
-                (first_ref.at[0], plus_recv.at[0, 0], z_next),
-                (first_ref.at[1], minus_recv.at[0, 1], z_prev),
-            )
-        else:
-            pairs = (
-                (plus_recv.at[s - 1], plus_recv.at[s], z_next),
-                (minus_recv.at[s - 1], minus_recv.at[s], z_prev),
-            )
-        return [
-            remote(src, dst, ring_send.at[s, n], ring_rsem.at[s, n], peer)
-            for n, (src, dst, peer) in enumerate(pairs)
-        ]
-
-    def ring_step(s):
-        zp = lax.rem(zed + 4 - s, N_Z)
-        zm = lax.rem(zed + 4 + s, N_Z)
-        copies = ring_copies(s)
-        if s == 0:
-            core_copy(0).wait_recv()
-            for y in range(2):
-                first_ref[y] = low(chip_sum(zp, y))
-                copies[y].start()
-            return
-        earlier = ring_copies(s - 1)
-        core_copy(2 * s - 1).wait_recv()
-        earlier[0].wait_recv()
-        for y in range(2):
-            value = chip_sum(zp, y)
-            if s > 1 or y == 0:
-                value = value + f32(plus_recv[s - 1, y])
-            plus_recv[s - 1, y] = low(value)
-        copies[0].start()
-        core_copy(2 * s).wait_recv()
-        earlier[1].wait_recv()
-        for y in range(2):
-            value = chip_sum(zm, y)
-            if s > 1 or y == 1:
-                value = value + f32(minus_recv[s - 1, y])
-            minus_recv[s - 1, y] = low(value)
-        copies[1].start()
+    streams = ((plus_recv, z_next, -1), (minus_recv, z_prev, 1))
+
+    def ring_copy(d, stream, hop):
+        recv, peer, _ = streams[d]
+        y = d if stream == 0 else 1 - d
+        start = 0 if stream == 0 else 1
+        src = first_ref.at[d, stream] if hop == start else recv.at[hop - 1, y]
+        return remote(
+            src, recv.at[hop, y], ring_send.at[d, stream, hop], ring_rsem.at[d, stream, hop], peer
+        )
+
+    def ring_step(stream, hop):
+        start = 0 if stream == 0 else 1
+        for d in range(2):
+            recv, _, sign = streams[d]
+            y = d if stream == 0 else 1 - d
+            z = lax.rem(zed + 4 + sign * hop, N_Z)
+            if stream == 1:
+                core_copy(2 * hop - 1 + d).wait_recv()
+            elif hop == 0 and d == 0:
+                core_copy(0).wait_recv()
+            if hop == start:
+                first_ref[d, stream] = low(chip_sum(z, y))
+            else:
+                ring_copy(d, stream, hop - 1).wait_recv()
+                recv[hop - 1, y] = low(chip_sum(z, y) + f32(recv[hop - 1, y]))
+            ring_copy(d, stream, hop).start()
 
     def pair(i, carry):
         z = core_z(i)
@@ -314,7 +304,7 @@
             zero = jnp.zeros_like(ds[0])
             ds_t, p_t = [], []
             for e in range(NSET):
-                hit = [ids_ref[n : n + 1, :] == e for n in range(NBR)]
+                hit = [hits[n][e] for n in range(NBR)]
                 ds_t.append(low(jnp.where(hit[0], ds[0], zero) + jnp.where(hit[1], ds[1], zero)))
                 p_t.append(low(jnp.where(hit[0], pb[0], zero) + jnp.where(hit[1], pb[1], zero)))
             ds_t = jnp.concatenate(ds_t, axis=0)
@@ -333,86 +323,101 @@
                 at = (2 * y + c) * HEAD
                 dw_ref[c, z, y] = dw[at : at + HEAD]
         core_copy(i).start()
-        for s in range(4):
-
-            @pl.when(i == 2 * s + 1)
-            def _(s=s):
-                ring_step(s)
+        for at, stream, hop in ((1, 0, 0), (3, 1, 1), (5, 0, 1)):
+
+            @pl.when(i == at)
+            def _(stream=stream, hop=hop):
+                ring_step(stream, hop)
 
         return carry
 
     lax.fori_loop(0, N_Z, pair, 0)
-
-    sec_copies = []
+    ring_step(1, 2)
+
+    sec_copies = [[], []]
     for half in range(2):
         rows = pl.ds(half * 2 * NLEN, 2 * NLEN)
-        de_ref[2 * half : 2 * half + 2] = low(dot_nn(gs_ref[rows, :], w_ref[...])).reshape(
-            2, NLEN, ENC_D
-        )
+        two = slice(2 * half, 2 * half + 2)
+        de_ref[two] = low(dot_nn(gs_ref[rows, :], w_ref[...])).reshape(2, NLEN, ENC_D)
         for i, peer in enumerate(sec):
             copy = remote(
-                de_ref.at[2 * half : 2 * half + 2, row_slot(targets[i]), :],
-                de_recv.at[i, 2 * half : 2 * half + 2],
+                de_ref.at[two, row_slot(targets[i]), :],
+                de_recv.at[i, two],
                 sec_send.at[half, i],
                 sec_rsem.at[half, i],
                 peer,
             )
             copy.start()
-            sec_copies.append(copy)
-
-    normed, inverse = encode(x_ref[...].reshape(NSET * LOCAL, ENC_D), encw_ref[...])
+            sec_copies[half].append(copy)
+
+    normed_rows, inverse_rows = encode(x_ref[...].reshape(NSET * LOCAL, ENC_D), encw_ref[...])
     xt_ref[...] = x_all[...].reshape(ROWS, ENC_D).T
-
-    core_copy(N_Z - 1).wait_recv()
-    for copy in ring_copies(3):
-        copy.wait_recv()
-    for y in range(2):
-        fin_ref[y] = low(chip_sum(zed, y) + f32(plus_recv[3, y]) + f32(minus_recv[3, y]))
-    y_copy = remote(fin_ref.at[1 - yhi], y_recv, y_send, y_rsem, y_peer)
-    y_copy.start()
-
-    for copy in sec_copies:
-        copy.wait_recv()
-    grad = f32(de_ref[:, row_slot(me), :])
-    for i in range(N_SEC - 1):
-        grad = grad + f32(de_recv[i])
-    grad = grad.reshape(NSET * LOCAL, ENC_D)
-    grad_normed = grad * gain_ref[...]
-    grad_mixed = inverse * (
-        grad_normed - normed * jnp.mean(grad_normed * normed, axis=-1, keepdims=True)
-    )
-    grad_low = low(grad_mixed)
-    low_loc[...] = grad_low.reshape(NSET, LOCAL, ENC_D)
-    low_copies = []
-    for i, peer in enumerate(sec):
-        copy = remote(
-            low_loc, low_all.at[:, row_slot(me), :], low_send.at[i], low_rsem.at[i], peer
-        )
-        copy.start()
-        low_copies.append(copy)
-    gain_row = jnp.sum(grad * normed, axis=0, keepdims=True)
+    ring_step(0, 2)
+
+    low_copies = [[], []]
+    mixed_parts, low_parts = [], []
+    gain_row = jnp.zeros((1, ENC_D), jnp.float32)
+    for half in range(2):
+        two = slice(2 * half, 2 * half + 2)
+        own = slice(2 * LOCAL * half, 2 * LOCAL * (half + 1))
+        normed, inverse = normed_rows[own], inverse_rows[own]
+        for copy in sec_copies[half]:
+            copy.wait_recv()
+        grad = f32(de_ref[two, row_slot(me), :])
+        for i in range(N_SEC - 1):
+            grad = grad + f32(de_recv[i, two])
+        grad = grad.reshape(2 * LOCAL, ENC_D)
+        grad_normed = grad * gain
+        grad_mixed = inverse * (
+            grad_normed - normed * jnp.mean(grad_normed * normed, axis=-1, keepdims=True)
+        )
+        grad_low = low(grad_mixed)
+        low_loc[two] = grad_low.reshape(2, LOCAL, ENC_D)
+        for i, peer in enumerate(sec):
+            copy = remote(
+                low_loc.at[two],
+                low_all.at[two, row_slot(me), :],
+                low_send.at[half, i],
+                low_rsem.at[half, i],
+                peer,
+            )
+            copy.start()
+            low_copies[half].append(copy)
+        low_all[two, row_slot(me), :] = low_loc[two]
+        gain_row = gain_row + jnp.sum(grad * normed, axis=0, keepdims=True)
+        mixed_parts.append(grad_mixed)
+        low_parts.append(grad_low)
     gain_loc[...] = jnp.concatenate(
         [gain_row[:, i * 128 : (i + 1) * 128] for i in range(7)]
         + [jnp.zeros((1, 128), jnp.float32)],
         axis=0,
     )
+    gain_copies = []
     for i, peer in enumerate(sec):
         copy = remote(gain_loc, gain_all.at[i], gn_send.at[i], gn_rsem.at[i], peer)
         copy.start()
-        low_copies.append(copy)
-    low_all[:, row_slot(me), :] = low_loc[...]
-    embed = grad_mixed + dot_nt(grad_low, encw_ref[...])
+        gain_copies.append(copy)
+    embed = jnp.concatenate(mixed_parts, axis=0) + dot_nt(
+        jnp.concatenate(low_parts, axis=0), encw_ref[...]
+    )
     eg_ref[...] = low(embed).reshape(NSET, LOCAL, ENC_D)
-
-    y_copy.wait_recv()
-    kvg_ref[...] = f32(fin_ref[yhi]) + f32(y_recv[...])
-
-    for copy in low_copies:
+    ring_step(1, 3)
+
+    mine = pl.ds(pl.multiple_of(me * OWN_ROWS, 16), OWN_ROWS)
+    weight = None
+    for half in range(2):
+        two = slice(2 * half, 2 * half + 2)
+        for copy in low_copies[half]:
+            copy.wait_recv()
+        part = dot_nn(
+            xt_ref[mine, 2 * NLEN * half : 2 * NLEN * (half + 1)],
+            low_all[two].reshape(2 * NLEN, ENC_D),
+        )
+        weight = part if half == 0 else weight + part
+        if half == 0:
+            ring_step(0, 3)
+    for copy in gain_copies:
         copy.wait_recv()
-    weight = dot_nn(
-        xt_ref[pl.ds(pl.multiple_of(me * OWN_ROWS, 16), OWN_ROWS), :],
-        low_all[...].reshape(ROWS, ENC_D),
-    )
     gain_sum = gain_loc[...]
     for i in range(N_SEC - 1):
         gain_sum = gain_sum + gain_all[i]
@@ -452,6 +457,14 @@
         )
         copy.start()
         z_copies.append(copy)
+    core_copy(N_Z - 1).wait_recv()
+    for d in range(2):
+        for stream in range(2):
+            ring_copy(d, stream, 3).wait_recv()
+    for y in range(2):
+        fin_ref[y] = low(chip_sum(zed, y) + f32(plus_recv[3, y]) + f32(minus_recv[3, y]))
+    y_copy = remote(fin_ref.at[1 - yhi], y_recv, y_send, y_rsem, y_peer)
+    y_copy.start()
     total = f32(zp_ref[zed])
     for i in range(N_Z - 1):
         z_copies[i].wait_recv()
@@ -463,6 +476,8 @@
         copy.start()
         za_copies.append(copy)
     za_all[zed] = za_ref[...]
+    y_copy.wait_recv()
+    kvg_ref[...] = f32(fin_ref[yhi]) + f32(y_recv[...])
     for copy in za_copies:
         copy.wait_recv()
     wa_copies = []
@@ -473,14 +488,18 @@
     wa_all[my_quad] = za_all[...]
 
     y_copy.wait_send()
-    for group in (x_copies, sec_copies, low_copies, quad_copies, z_copies, za_copies):
+    for group in [x_copies, gain_copies, quad_copies, z_copies, za_copies] + (
+        sec_copies + low_copies
+    ):
         for copy in group:
             copy.wait_send()
     for i in range(N_Z):
         core_copy(i).wait_send()
-    for s in range(4):
-        for copy in ring_copies(s):
-            copy.wait_send()
+    for d in range(2):
+        for hop in range(4):
+            ring_copy(d, 0, hop).wait_send()
+            if hop > 0:
+                ring_copy(d, 1, hop).wait_send()
 
     for copy in wa_copies:
         copy.wait_recv()
@@ -523,7 +542,7 @@
             vmem((ROWS, 2 * width), bf),
             vmem((2, N_Z, 2, HEAD, ENC_D), bf),
             vmem((N_Z, 2, HEAD, ENC_D), bf),
-            vmem((2, HEAD, ENC_D), bf),
+            vmem((2, 2, HEAD, ENC_D), bf),
             vmem((4, 2, HEAD, ENC_D), bf),
             vmem((4, 2, HEAD, ENC_D), bf),
             vmem((2, HEAD, ENC_D), bf),
@@ -546,14 +565,14 @@
             dma((7,)),
             dma((8,)),
             dma((8,)),
-            dma((4, 2)),
-            dma((4, 2)),
+            dma((2, 2, 4)),
+            dma((2, 2, 4)),
             dma,
             dma,
             dma((2, 7)),
             dma((2, 7)),
-            dma((7,)),
-            dma((7,)),
+            dma((2, 7)),
+            dma((2, 7)),
             dma((7,)),
             dma((7,)),
             dma((3,)),
@@ -572,40 +591,56 @@
     )(ids, x_local, gain, enc_weight, kv_weight, queries, pos_bias, ctx_grad)
 
 
-def finish_kernel(q_in, k_in, w_in, g_in, e_in, q_out, k_out, w_out, g_out, e_out):
-    q_out[...] = q_in[...]
-    k_out[...] = k_in[...]
-    w_out[...] = w_in[...]
+def finish_kernel(*refs):
+    ins, outs, holds = refs[:4], refs[5:9], refs[10:14]
+    g_in, g_out = refs[4], refs[9]
+    in_sem, out_sem = refs[14], refs[15]
+    fetch = [
+        pltpu.make_async_copy(a, b, in_sem.at[i]) for i, (a, b) in enumerate(zip(ins, holds))
+    ]
+    store = [
+        pltpu.make_async_copy(a, b, out_sem.at[i]) for i, (a, b) in enumerate(zip(holds, outs))
+    ]
+    for copy in fetch:
+        copy.start()
     for i in range(7):
-        g_out[:, i * 128 : (i + 1) * 128] = g_in[i : i + 1, :]
-    e_out[...] = e_in[...]
-
-
-def finish(outs):
-    shapes = [jax.ShapeDtypeStruct(o.shape, o.dtype) for o in outs]
-    shapes[3] = jax.ShapeDtypeStruct((1, ENC_D), jnp.float32)
+        g_out[i * 128 : (i + 1) * 128] = g_in[i]
+    for a, b in zip(fetch, store):
+        a.wait()
+        b.start()
+    for copy in store:
+        copy.wait()
+
+
+def finish(q_grad, kv_grad, w_grad, g_grad, e_grad):
+    bulk = [q_grad, kv_grad, w_grad, e_grad]
+    any_spec = pl.BlockSpec(memory_space=pl.ANY)
     return pl.pallas_call(
         finish_kernel,
-        out_shape=shapes,
-        in_specs=[VMEM_SPEC] * 5,
-        out_specs=[VMEM_SPEC] * 5,
+        out_shape=[jax.ShapeDtypeStruct(o.shape, o.dtype) for o in bulk]
+        + [jax.ShapeDtypeStruct((ENC_D,), jnp.float32)],
+        in_specs=[any_spec] * 4 + [VMEM_SPEC],
+        out_specs=[any_spec] * 4 + [VMEM_SPEC],
+        scratch_shapes=[pltpu.VMEM(o.shape, o.dtype) for o in bulk]
+        + [pltpu.SemaphoreType.DMA((4,)), pltpu.SemaphoreType.DMA((4,))],
+        compiler_params=pltpu.CompilerParams(vmem_limit_bytes=62 * 1024 * 1024),
         name="finish",
-    )(*outs)
+    )(*bulk, g_grad)
 
 
 def body(nbr_embed, enc_weight, enc_gain, kv_weight, queries, pos_bias, nbr_ids, ctx_grad):
     outs = train(
-        jnp.repeat(nbr_ids[0].T, BLOCK, axis=1),
+        nbr_ids,
         nbr_embed[0],
-        enc_gain[None, :],
+        enc_gain,
         enc_weight,
         kv_weight,
         queries,
         pos_bias,
         ctx_grad,
     )
-    q_grad, kv_grad, w_grad, g_grad, e_grad = finish(outs)
-    return (q_grad, kv_grad[None], w_grad, g_grad.reshape(ENC_D), e_grad[None])
+    q_grad, kv_grad, w_grad, e_grad, g_grad = finish(*outs)
+    return (q_grad, kv_grad[None], w_grad, g_grad, e_grad[None])
 
 
 def solution(mesh):

time: 114 us -> 92.6 us (0.81)
  Pallas kernels: 109 us -> 91.8 us
  local copies, waits for them, and re-layouts: 2.75 us -> 0 us
  other arithmetic: 1.27 us -> 0 us
    pallas_call x1, Pallas kernels: 107 us -> 88.4 us  [train(): pl.pallas_call(train_kernel, out_shape=[jax.ShapeDtypeStruct((1, TOK_DEV,...]
    broadcast_in_dim x2 -> x0, local copies, waits for them, and re-layouts: 1.34 us -> none  [the longest x1 1.27 us: body(): enc_gain[None, :]]
    pallas_call x1 -> x0, other arithmetic: 1.27 us -> none  [finish(): pl.pallas_call(finish_kernel, out_shape=shapes, in_specs=[VMEM_SPEC] * 5,...]
where the time goes in v2:
time: 92.6 us; the launch traced here: 92.5 us
  Pallas kernels  91.8 us (99%)
    pallas_call x1, Pallas kernels, train(): pl.pallas_call(train_kernel, out_shape=[jax.ShapeDtypeStruct((1, TOK_DEV,...  88.4 us
    pallas_call x1, Pallas kernels, finish(): pl.pallas_call(finish_kernel, out_shape=[jax.ShapeDtypeStruct(o.shape, o....  3.46 us

profile of v2, /device:TPU:1, one launch (start us, length us, event | category | flops | bytes accessed | tf_op | source)
XLA Modules:
  0.0 92.5 jit_solution(14117702925616739224)
XLA Ops:
  0.6 88.4 %train.1 = (bf16[1,128,2048]{2,1,0:T(8,128)(2,1)}, f32[128,896]{1,0:T(8,128)}, f32[112,896]{1,0:T(8,128)}, f32[8,128]{1,0:T(8,128)}, bf16[4,16,896]{2,1,0:T(8,128)(2,1)}) custom-call(s32[1,2,2]{2,1,0:T(2,128)} %ids_ref.1, bf16[4,16,896]{2,1,0:T(8,128)(2,1)} %bitcast.3, f32[896]{0:T(1024)} %gain_ref.1, bf16[896,896]{1,0:T(8,128)(2,1)} %encw_hbm.1, ...), custom_call_target="tpu_custom_call" | custom-call | tf_op jit(solution)/shard_map/train/pallas_call | solution.py:522
  89.0 3.5 %finish.1 = (bf16[1,128,2048]{2,1,0:T(8,128)(2,1)}, f32[128,896]{1,0:T(8,128)}, f32[112,896]{1,0:T(8,128)}, bf16[4,16,896]{2,1,0:T(8,128)(2,1)}, f32[896]{0:T(1024)}) custom-call(bf16[1,128,2048]{2,1,0:T(8,128)(2,1)} %get-tuple-element.15.refs_0_, f32[128,896]{1,0:T(8,128)} %get-tuple-element.16.refs_1_, f32[112,896]{1,0:T(8,128)} %get-tuple-element.17.refs_2_, ...), custom_call_target="tpu_custom_call" | custom-call | tf_op jit(solution)/shard_map/finish/pallas_call | solution.py:618
